TPU v7x, 32 devices: a whole 2x2x4 slice. The times are simulated.
32 devices in a mesh: grp: 2 (over core), seq: 4 (over y, x), row: 4 (over z).
Axes of the slice: x: 2, y: 2, z: 4, core: 2. Of those that a mesh axis runs over, the one named last changes fastest.
Arguments:
- tokens: bfloat16 [512, 70, 1150], P(('grp', 'seq')), may hold values from -6 to 6
- in_mask: int32 [512, 1150], P(('grp', 'seq')), may hold values 0 or 1
- out_mask: int32 [512, 400], P(('grp', 'seq')), may hold values 0 or 1
- lengths: int32 [512], P(('grp', 'seq')), may hold values from 35 to 70, as said below
- groups: int32 [512], P(('grp', 'seq')), may hold values from 0 to 1, as said below
- input_gate_weight: bfloat16 [1600, 1150], P('row'), may hold values from -0.1875 to 0.1875
- w_recur: bfloat16 [1600, 400], P('row'), may hold values from -0.3125 to 0.3125
- weight_mask: int32 [1600, 400], P('row'), may hold values 0 or 1
- bias: float32 [1600], P('row'), may hold values from -3 to 3
- cotangent: bfloat16 [512, 70, 400], P(('grp', 'seq')), may hold values from -6 to 6
Outputs:
- input_grad: float32 [512, 70, 1150], P(('grp', 'seq', 'row'))
- grad_input_weight: float32 [2, 1600, 1150], P('grp', 'row')
- grad_recur_weight: float32 [2, 1600, 400], P('grp', 'row')
- grad_bias: float32 [2, 1600], P('grp', 'row')
- gram: float32 [2, 2], replicated
Inputs may be any that keep to these rules, and one draw needn't show every extreme that they name: `lengths`: each sequence has the full length or fewer steps; some sequence of the batch has exactly 70 steps and some exactly 35. Both groups have sequences.
All inputs are finite; a program needn't handle non-finite values. No bound on the sum of `in_mask` or of `out_mask` or of `weight_mask` on one device may be relied on, other than what follows from the above.
Results may differ from a plain program's by a relative error of at most 0.0063.
Values may be sent and summed in bfloat16 or wider, within the bound.
No kernel may reach another device: no remote copies, remote signals or barrier semaphores. Data moves between devices by JAX's collectives and lax.ppermute only.
A program may use at most 256 MiB of HBM per device.

v0:
```python
import jax
import jax.numpy as jnp
from jax import lax
from jax.sharding import PartitionSpec as P

ACTIVATION_COEF = 2.0
TAR_BETA = 1.0
KEEP_INPUT = 0.75
KEEP_OUTPUT = 0.6
KEEP_WEIGHT = 0.5


def swapped(block, axis, stride):
    count = lax.axis_size(axis)
    route = []
    for low in range(count):
        high = low | 1 << stride
        if high != low and high < count:
            route += [(low, high), (high, low)]
    return lax.ppermute(block, axis, route)


def gate_split(values, hidden):
    return (
        jax.nn.sigmoid(values[:, :hidden]),
        jax.nn.sigmoid(values[:, hidden : 2 * hidden]),
        jnp.tanh(values[:, 2 * hidden : 3 * hidden]),
        jax.nn.sigmoid(values[:, 3 * hidden :]),
    )


def local(
    tokens,
    in_mask,
    out_mask,
    lengths,
    groups,
    input_gate_weight,
    w_recur,
    weight_mask,
    bias,
    cotangent,
):
    seq_count, time_steps, width_in = tokens.shape
    hidden = cotangent.shape[2]
    row_count = input_gate_weight.shape[0]
    row_start = lax.axis_index("row") * row_count
    share = seq_count // lax.axis_size("row")
    share_start = lax.axis_index("row") * share
    group_hot = (groups[:, None] == jnp.arange(2)[None, :]).astype(jnp.float32)
    valid_mask = (jnp.arange(time_steps)[None, :] < lengths[:, None]).astype(jnp.float32)
    local_counts = jnp.sum(group_hot * jnp.sum(valid_mask, 1)[:, None], 0)
    counts = lax.psum(local_counts, ("grp", "seq"))
    group_ratio = jnp.sum(counts) / counts
    seq_ratio = jnp.sum(group_hot * group_ratio[None, :], 1)
    in_scale = in_mask.astype(jnp.float32) / KEEP_INPUT
    dropped_weight = (tokens.astype(jnp.float32) * in_scale[:, None, :]).astype(jnp.bfloat16)
    w_scale = weight_mask.astype(jnp.float32) / KEEP_WEIGHT
    w_eff = (w_recur.astype(jnp.float32) * w_scale).astype(jnp.bfloat16)
    projected = (
        jnp.einsum(
            "thw,aw->hta", dropped_weight, input_gate_weight, preferred_element_type=jnp.float32
        )
        + bias[None, None, :]
    )
    zero_state = jnp.zeros((seq_count, hidden), jnp.float32)

    def full_gates(proj_step, hidden_low):
        partial_gates = proj_step + jnp.einsum(
            "sh,rh->sr", hidden_low, w_eff, preferred_element_type=jnp.float32
        )
        return lax.all_gather(partial_gates, "row", axis=1, tiled=True)

    def recur_back(pre_grad):
        own_rows = lax.dynamic_slice_in_dim(pre_grad, row_start, row_count, 1)
        partial_back = jnp.dot(own_rows, w_eff, preferred_element_type=jnp.float32)
        return lax.psum(partial_back, "row")

    def forward_step(carry, proj_step):
        cell_state, hidden_low = carry
        pre_act = full_gates(proj_step, hidden_low)
        gate_input_part, gate_forget, gate_cell, gate_output_part = gate_split(pre_act, hidden)
        new_cell = gate_forget * cell_state + gate_input_part * gate_cell
        new_hidden = gate_output_part * jnp.tanh(new_cell)
        stored = jnp.concatenate([gate_input_part, gate_forget, gate_cell, gate_output_part], 1)
        return ((new_cell, new_hidden.astype(jnp.bfloat16)), (stored, new_cell, new_hidden))

    start_state = (zero_state, zero_state.astype(jnp.bfloat16))
    _, (activations, cell_seq, hidden_seq) = lax.scan(forward_step, start_state, projected)
    out_scale = out_mask.astype(jnp.float32) / KEEP_OUTPUT
    cot_time = jnp.swapaxes(cotangent, 0, 1).astype(jnp.float32)
    valid_time = valid_mask.T
    outputs = hidden_seq * out_scale[None]
    out_grad = valid_time[:, :, None] * (
        cot_time + 2.0 * ACTIVATION_COEF * seq_ratio[None, :, None] * outputs
    )
    zero_row = jnp.zeros((1, seq_count, hidden), jnp.float32)
    hidden_prev = jnp.concatenate([zero_row, hidden_seq[:-1]], 0)
    later = (jnp.arange(time_steps) >= 1).astype(jnp.float32)
    smooth_weight = 2.0 * TAR_BETA * seq_ratio[None, :] * valid_time * later[:, None]
    smooth_term = smooth_weight[:, :, None] * (hidden_seq - hidden_prev)
    direct_grad = (
        out_grad * out_scale[None] + smooth_term - jnp.concatenate([smooth_term[1:], zero_row], 0)
    )
    cell_prev = jnp.concatenate([zero_row, cell_seq[:-1]], 0)

    def backward_step(carry, inputs_now):
        cell_grad, recur_grad = carry
        direct_now, stored, cell_state, cell_before = inputs_now
        gate_input_part = stored[:, :hidden]
        gate_forget = stored[:, hidden : 2 * hidden]
        gate_cell = stored[:, 2 * hidden : 3 * hidden]
        gate_output_part = stored[:, 3 * hidden :]
        hidden_grad = direct_now + recur_grad
        tanh_cell = jnp.tanh(cell_state)
        total_cell = cell_grad + hidden_grad * gate_output_part * (1.0 - tanh_cell * tanh_cell)
        pre_grad = jnp.concatenate(
            [
                total_cell * gate_cell * gate_input_part * (1.0 - gate_input_part),
                total_cell * cell_before * gate_forget * (1.0 - gate_forget),
                total_cell * gate_input_part * (1.0 - gate_cell * gate_cell),
                hidden_grad * tanh_cell * gate_output_part * (1.0 - gate_output_part),
            ],
            1,
        ).astype(jnp.bfloat16)
        own_rows = lax.dynamic_slice_in_dim(pre_grad, row_start, row_count, 1)
        share_rows = lax.dynamic_slice_in_dim(pre_grad, share_start, share, 0)
        new_carry = (total_cell * gate_forget, recur_back(pre_grad))
        return (new_carry, (own_rows, share_rows[:, :0]))

    _, (pre_grads, share_grads) = lax.scan(
        backward_step,
        (zero_state, zero_state),
        (direct_grad, activations, cell_seq, cell_prev),
        reverse=True,
    )
    grad_seq = jnp.swapaxes(pre_grads, 0, 1)
    prev_low = jnp.swapaxes(hidden_prev, 0, 1).astype(jnp.bfloat16)
    grads_in = []
    grads_rec = []
    bias_gradient_rows = []
    for group_index in range(2):
        selector = (groups == group_index).astype(jnp.bfloat16)
        masked = grad_seq * selector[:, None, None]
        grads_in.append(
            jnp.einsum("slr,slk->rk", masked, dropped_weight, preferred_element_type=jnp.float32)
        )
        grads_rec.append(
            jnp.einsum("slr,slh->rh", masked, prev_low, preferred_element_type=jnp.float32)
            * w_scale
        )
        bias_gradient_rows.append(jnp.sum(masked.astype(jnp.float32), (0, 1)))
    stacked = (jnp.stack(grads_in), jnp.stack(grads_rec), jnp.stack(bias_gradient_rows))
    own_scale = lax.dynamic_slice_in_dim(in_scale, share_start, share, 0)
    input_sum = lax.psum_scatter(
        jnp.einsum("slr,rk->slk", grad_seq, input_gate_weight, preferred_element_type=jnp.float32),
        "row",
        scatter_dimension=0,
        tiled=True,
    )
    input_grad = input_sum * own_scale[:, None, :]
    own_grads = (
        lax.psum_scatter(stacked[0], "grp", scatter_dimension=0, tiled=True),
        lax.psum_scatter(stacked[1], "grp", scatter_dimension=0, tiled=True),
        lax.psum_scatter(stacked[2], "grp", scatter_dimension=0, tiled=True),
    )
    own_grads = lax.psum((own_grads[0], own_grads[1], own_grads[2]), "seq")
    flat_own = jnp.concatenate([member.reshape(-1) for member in own_grads])
    flat_peer = swapped(flat_own.astype(jnp.bfloat16), "grp", 0).astype(flat_own.dtype)
    self_dot = jnp.sum(flat_own * flat_own)
    cross_dot = jnp.sum(flat_own * flat_peer)
    mine_hot = (jnp.arange(2) == lax.axis_index("grp")).astype(jnp.float32)
    local_gram = (
        mine_hot[:, None] * mine_hot[None, :] * self_dot
        + mine_hot[:, None] * (1.0 - mine_hot)[None, :] * cross_dot
    )
    gram = lax.psum(local_gram, ("grp", "row"))
    grad_in, grad_rec, grad_bias = own_grads
    return (input_grad, grad_in, grad_rec, grad_bias, gram)


def solution(mesh):
    return jax.shard_map(
        local,
        mesh=mesh,
        in_specs=(
            P(("grp", "seq"), None, None),
            P(("grp", "seq"), None),
            P(("grp", "seq"), None),
            P(("grp", "seq")),
            P(("grp", "seq")),
            P("row", None),
            P("row", None),
            P("row", None),
            P("row"),
            P(("grp", "seq"), None, None),
        ),
        out_specs=(
            P(("grp", "seq", "row"), None, None),
            P("grp", "row", None),
            P("grp", "row", None),
            P("grp", "row"),
            P(),
        ),
        check_vma=False,
    )
```

profile of v0, /device:TPU:0, one launch (start us, length us, event | category | flops | bytes accessed | tf_op | source)
XLA Modules:
  0.0 4704.8 jit_solution(5779984104247842560)
XLA Ops:
  33.6 1464.2 %while.38 = (s32[]{:T(128)}, f32[64,400]{1,0:T(8,128)S(1)}, bf16[64,400]{1,0:T(8,128)(2,1)S(1)}, f32[70,64,1600]{2,1,0:T(8,128)}, f32[70,64,400]{2,1,0:T(8,128)}...) while((s32[]{:T(128)}, f32[64,400]{1,0:T(8,128)S(1)}, ...), condition=%wide.region_6.7_spmd.clone, body=%wide.region_5.6_spmd.clone.sunk | while | flops 21171204 | bytes 6539380 | solution.py:89
  1561.2 2708.6 %while.39 = (s32[]{:T(128)}, f32[64,400]{1,0:T(8,128)S(1)}, f32[64,400]{1,0:T(8,128)}, bf16[70,64,400]{2,1,0:T(8,128)(2,1)}, f32[70,64,400]{2,1,0:T(8,128)}, /*i...) while((s32[]{:T(128)}, f32[64,400]{1,0:T(8,128)S(1)}, ...), condition=%wide.region_9.10_spmd.clone, body=%wide.region_7.9_spmd.clone.sunk | while | flops 21222404 | bytes 4233935 | solution.py:131
  1566.3 35.4 all-reduce.10.cloned.1.call-done
  1645.4 33.6 all-reduce.10.cloned.1.call-done
  1684.1 33.6 all-reduce.10.cloned.1.call-done
  1722.8 33.6 all-reduce.10.cloned.1.call-done
  1800.1 33.6 all-reduce.10.cloned.1.call-done
  1838.8 33.6 all-reduce.10.cloned.1.call-done
  1877.4 33.6 all-reduce.10.cloned.1.call-done
  1954.8 33.6 all-reduce.10.cloned.1.call-done
  1993.4 33.6 all-reduce.10.cloned.1.call-done
  2032.1 33.6 all-reduce.10.cloned.1.call-done
  2109.4 33.6 all-reduce.10.cloned.1.call-done
  2148.1 33.6 all-reduce.10.cloned.1.call-done
  2186.8 33.6 all-reduce.10.cloned.1.call-done
  2264.1 33.6 all-reduce.10.cloned.1.call-done
  2302.8 33.6 all-reduce.10.cloned.1.call-done
  2341.5 33.6 all-reduce.10.cloned.1.call-done
  2418.8 33.6 all-reduce.10.cloned.1.call-done
  2457.5 33.6 all-reduce.10.cloned.1.call-done
  2496.1 33.6 all-reduce.10.cloned.1.call-done
  2573.5 33.6 all-reduce.10.cloned.1.call-done
  2612.1 33.6 all-reduce.10.cloned.1.call-done
  2650.8 33.6 all-reduce.10.cloned.1.call-done
  2728.1 33.6 all-reduce.10.cloned.1.call-done
  2766.8 33.6 all-reduce.10.cloned.1.call-done
  2805.5 33.6 all-reduce.10.cloned.1.call-done
  2882.8 33.6 all-reduce.10.cloned.1.call-done
  2921.5 33.6 all-reduce.10.cloned.1.call-done
  2960.2 33.6 all-reduce.10.cloned.1.call-done
  3037.5 33.6 all-reduce.10.cloned.1.call-done
  3076.2 33.6 all-reduce.10.cloned.1.call-done
  3114.9 33.6 all-reduce.10.cloned.1.call-done
  3192.2 33.6 all-reduce.10.cloned.1.call-done
  3230.9 33.6 all-reduce.10.cloned.1.call-done
  3269.5 33.6 all-reduce.10.cloned.1.call-done
  3346.9 33.6 all-reduce.10.cloned.1.call-done
  3501.5 33.6 all-reduce.10.cloned.1.call-done
  3578.9 33.6 all-reduce.10.cloned.1.call-done
  3656.2 33.6 all-reduce.10.cloned.1.call-done
  3694.9 33.6 all-reduce.10.cloned.1.call-done
  3733.6 33.6 all-reduce.10.cloned.1.call-done
  3810.9 33.6 all-reduce.10.cloned.1.call-done
  3965.6 33.6 all-reduce.10.cloned.1.call-done
  4120.2 33.6 all-reduce.10.cloned.1.call-done
  4197.6 33.6 all-reduce.10.cloned.1.call-done
  4355.0 47.3 %all-reduce.8.cloned.1.call-done = (f32[1,400,1150]{2,1,0:T(8,128)}, f32[1,400,400]{2,1,0:T(8,128)}) async-done(((f32[1,400,1150]{2,1,0:T(8,128)}, f32[1,400,400]{2,1,0:T(8,128)}), (f32[1,400,1150]{2,1,0:T(8,128)}, f32[1,400,400]{2,1,0:T(8,128)})) %all-reduce.8.cloned.1.call-update) | async-done | bytes 2480016 | tf_op jit(solution)/shard_map/psum | solution.py:167
  4456.9 232.0 %reduce-scatter.4.cloned.1.call-done = f32[16,70,1150]{2,1,0:T(8,128)} async-done(((f32[64,70,1150]{2,1,0:T(8,128)}), f32[16,70,1150]{2,1,0:T(8,128)}) %reduce-scatter.4.cloned.1.call-update) | async-done | bytes 5152016 | tf_op jit(solution)/shard_map/reduce_scatter | solution.py:155
  (1381 shorter events, 2925.6 us)
Async XLA Ops:
  1561.2 40.5 all-reduce.10.cloned.1.call-start
  1640.3 38.7 all-reduce.10.cloned.1.call-start
  1679.0 38.7 all-reduce.10.cloned.1.call-start
  1717.6 38.7 all-reduce.10.cloned.1.call-start
  1795.0 38.7 all-reduce.10.cloned.1.call-start
  1833.6 38.7 all-reduce.10.cloned.1.call-start
  1872.3 38.7 all-reduce.10.cloned.1.call-start
  1949.6 38.7 all-reduce.10.cloned.1.call-start
  1988.3 38.7 all-reduce.10.cloned.1.call-start
  2027.0 38.7 all-reduce.10.cloned.1.call-start
  2104.3 38.7 all-reduce.10.cloned.1.call-start
  2143.0 38.7 all-reduce.10.cloned.1.call-start
  2181.7 38.7 all-reduce.10.cloned.1.call-start
  2259.0 38.7 all-reduce.10.cloned.1.call-start
  2297.7 38.7 all-reduce.10.cloned.1.call-start
  2336.4 38.7 all-reduce.10.cloned.1.call-start
  2413.7 38.7 all-reduce.10.cloned.1.call-start
  2452.4 38.7 all-reduce.10.cloned.1.call-start
  2491.0 38.7 all-reduce.10.cloned.1.call-start
  2568.4 38.7 all-reduce.10.cloned.1.call-start
  2607.0 38.7 all-reduce.10.cloned.1.call-start
  2645.7 38.7 all-reduce.10.cloned.1.call-start
  2723.0 38.7 all-reduce.10.cloned.1.call-start
  2761.7 38.7 all-reduce.10.cloned.1.call-start
  2800.4 38.7 all-reduce.10.cloned.1.call-start
  2877.7 38.7 all-reduce.10.cloned.1.call-start
  2916.4 38.7 all-reduce.10.cloned.1.call-start
  2955.1 38.7 all-reduce.10.cloned.1.call-start
  3032.4 38.7 all-reduce.10.cloned.1.call-start
  3071.1 38.7 all-reduce.10.cloned.1.call-start
  3109.7 38.7 all-reduce.10.cloned.1.call-start
  3187.1 38.7 all-reduce.10.cloned.1.call-start
  3225.7 38.7 all-reduce.10.cloned.1.call-start
  3264.4 38.7 all-reduce.10.cloned.1.call-start
  3380.4 38.7 all-reduce.10.cloned.1.call-start
  3419.1 38.7 all-reduce.10.cloned.1.call-start
  3535.1 38.7 all-reduce.10.cloned.1.call-start
  3573.8 38.7 all-reduce.10.cloned.1.call-start
  3689.8 38.7 all-reduce.10.cloned.1.call-start
  3728.5 38.7 all-reduce.10.cloned.1.call-start
  3844.5 38.7 all-reduce.10.cloned.1.call-start
  3883.1 38.7 all-reduce.10.cloned.1.call-start
  3999.1 38.7 all-reduce.10.cloned.1.call-start
  4037.8 38.7 all-reduce.10.cloned.1.call-start
  4153.8 38.7 all-reduce.10.cloned.1.call-start
  4192.5 38.7 all-reduce.10.cloned.1.call-start
  4307.5 94.8 %all-reduce.8.cloned.1.call-start = ((), (), s32[]{:S(2)}) async-start(), calls=%async_computation.6 | async-start | bytes 5324800 | tf_op jit(solution)/shard_map/psum | solution.py:167
  4318.8 370.2 %reduce-scatter.4.cloned.1.call-start = ((), (), s32[]{:S(2)}) async-start(), calls=%async_computation.3 | async-start | bytes 26542080 | tf_op jit(solution)/shard_map/reduce_scatter | solution.py:155
  (40 other events, 3130.9 us)
Sparse Core Ops, SparseCore 0:
  1565.7 35.9 all-reduce.9
  1644.8 34.1 all-reduce.9
  1683.5 34.1 all-reduce.9
  1722.1 34.1 all-reduce.9
  1799.5 34.1 all-reduce.9
  1838.1 34.1 all-reduce.9
  1876.8 34.1 all-reduce.9
  1954.1 34.1 all-reduce.9
  1992.8 34.1 all-reduce.9
  2031.5 34.1 all-reduce.9
  2108.8 34.1 all-reduce.9
  2147.5 34.1 all-reduce.9
  2186.2 34.1 all-reduce.9
  2263.5 34.1 all-reduce.9
  2302.2 34.1 all-reduce.9
  2340.9 34.1 all-reduce.9
  2418.2 34.1 all-reduce.9
  2456.9 34.1 all-reduce.9
  2495.5 34.1 all-reduce.9
  2572.9 34.1 all-reduce.9
  2611.5 34.1 all-reduce.9
  2650.2 34.1 all-reduce.9
  2727.5 34.1 all-reduce.9
  2766.2 34.1 all-reduce.9
  2804.9 34.1 all-reduce.9
  2882.2 34.1 all-reduce.9
  2920.9 34.1 all-reduce.9
  2959.6 34.1 all-reduce.9
  3036.9 34.1 all-reduce.9
  3075.6 34.1 all-reduce.9
  3114.2 34.1 all-reduce.9
  3191.6 34.1 all-reduce.9
  3230.2 34.1 all-reduce.9
  3268.9 34.1 all-reduce.9
  3346.2 34.1 all-reduce.9
  3384.9 34.1 all-reduce.9
  3423.6 34.1 all-reduce.9
  3500.9 34.1 all-reduce.9
  3539.6 34.1 all-reduce.9
  3578.3 34.1 all-reduce.9
  3655.6 34.1 all-reduce.9
  3694.3 34.1 all-reduce.9
  3733.0 34.1 all-reduce.9
  3810.3 34.1 all-reduce.9
  3849.0 34.1 all-reduce.9
  3965.0 34.1 all-reduce.9
  4119.6 34.1 all-reduce.9
  4335.8 353.1 reduce-scatter.3
  (23 shorter events, 783.4 us)
Sparse Core Ops, SparseCore 1:
  4284.4 8.7 reduce-scatter.7
  4307.6 11.1 reduce-scatter.5
  4322.2 80.1 all-reduce.7
where the time goes:
time: 4720 us; the launch traced here: 4700 us
  waiting for transfers between devices  2650 us (56%)
  blocking collectives  1150 us (24%)
  local copies, waits for them, and re-layouts  459 us (10%)
  other arithmetic  285 us (6%)
  matrix products  144 us (3%)
    psum x70, waiting for transfers between devices, recur_back(): return lax.psum(partial_back, 'row')  2350 us
    all_gather x70, blocking collectives, full_gates(): return lax.all_gather(partial_gates, 'row', axis=1, tiled=True)  1100 us
    reduce_scatter x1, waiting for transfers between devices, local(): lax.psum_scatter(jnp.einsum('slr,rk->slk', grad_seq, input_gate_weight, p...  232 us
    another operation x142, other arithmetic  156 us
    dynamic_update_slice x140, local copies, waits for them, and re-layouts, local(): lax.scan(forward_step, start_state, projected)  102 us
  transfers between devices with their start and end apart: 75, of which 74 were waited for; matrix products, arithmetic and copies ran while one was open for 3% of the time, Pallas kernels for 0%

commit v1 on v0

--- a/solution.py
+++ b/solution.py
@@ -74,7 +74,7 @@
     def recur_back(pre_grad):
         own_rows = lax.dynamic_slice_in_dim(pre_grad, row_start, row_count, 1)
         partial_back = jnp.dot(own_rows, w_eff, preferred_element_type=jnp.float32)
-        return lax.psum(partial_back, "row")
+        return jnp.sum(lax.all_gather(partial_back, "row"), axis=0)
 
     def forward_step(carry, proj_step):
         cell_state, hidden_low = carry

time: 4720 us -> 3430 us (0.73)
  waiting for transfers between devices: 2650 us -> 300 us
  blocking collectives: 1150 us -> 2260 us
    psum x70 -> x0, waiting for transfers between devices: 2350 us -> none  [recur_back(): return lax.psum(partial_back, 'row')]
    all_gather x0 -> x70, blocking collectives: none -> 1100 us  [recur_back(): return jnp.sum(lax.all_gather(partial_back, 'row'), axis=0)]
  transfers between devices with their start and end apart: 75 -> 5, of which waited for: 74 -> 4; matrix products, arithmetic and copies ran while one was open for 3% -> 2% of each run, Pallas kernels for 0% -> 0%
where the time goes in v1:
time: 3430 us; the launch traced here: 3420 us
  blocking collectives  2260 us (66%)
  local copies, waits for them, and re-layouts  454 us (13%)
  waiting for transfers between devices  300 us (9%)
  other arithmetic  285 us (8%)
  matrix products  97.2 us (3%)
    all_gather x70, blocking collectives, full_gates(): return lax.all_gather(partial_gates, 'row', axis=1, tiled=True)  1110 us
    all_gather x70, blocking collectives, recur_back(): return jnp.sum(lax.all_gather(partial_back, 'row'), axis=0)  1100 us
    reduce_scatter x1, waiting for transfers between devices, local(): lax.psum_scatter(jnp.einsum('slr,rk->slk', grad_seq, input_gate_weight, p...  234 us
    another operation x142, other arithmetic  152 us
    dynamic_update_slice x140, local copies, waits for them, and re-layouts, local(): lax.scan(forward_step, start_state, projected)  102 us
    dynamic_slice x70, local copies, waits for them, and re-layouts, local(): lax.scan(forward_step, start_state, projected)  93.5 us
    squeeze x70, local copies, waits for them, and re-layouts, local(): lax.scan(backward_step, (zero_state, zero_state), (direct_grad, activatio...  72.8 us
  transfers between devices with their start and end apart: 5, of which 4 were waited for; matrix products, arithmetic and copies ran while one was open for 2% of the time, Pallas kernels for 0%

profile of v1, /device:TPU:0, one launch (start us, length us, event | category | flops | bytes accessed | tf_op | source)
XLA Modules:
  0.0 3416.6 jit_solution(10839606858315069539)
XLA Ops:
  32.9 1468.5 %while.38 = (s32[]{:T(128)}, f32[64,400]{1,0:T(8,128)S(1)}, bf16[64,400]{1,0:T(8,128)(2,1)S(1)}, f32[70,64,1600]{2,1,0:T(8,128)}, f32[70,64,400]{2,1,0:T(8,128)}...) while((s32[]{:T(128)}, f32[64,400]{1,0:T(8,128)S(1)}, ...), condition=%wide.region_6.7_spmd.clone, body=%wide.region_5.6_spmd.clone.sunk | while | flops 21171204 | bytes 6539380 | solution.py:89
  34.6 17.4 all-gather.6
  57.1 16.3 all-gather.6
  119.1 16.2 all-gather.6
  140.4 16.6 all-gather.6
  162.2 16.5 all-gather.6
  245.8 16.4 all-gather.6
  267.4 16.6 all-gather.6
  289.1 16.6 all-gather.6
  373.0 16.3 all-gather.6
  394.5 16.5 all-gather.6
  416.1 16.6 all-gather.6
  499.7 16.4 all-gather.6
  521.3 16.6 all-gather.6
  543.0 16.7 all-gather.6
  626.7 16.3 all-gather.6
  648.2 16.4 all-gather.6
  669.7 16.6 all-gather.6
  753.3 16.2 all-gather.6
  774.6 16.8 all-gather.6
  796.6 16.5 all-gather.6
  880.4 16.2 all-gather.6
  901.7 16.6 all-gather.6
  923.4 16.6 all-gather.6
  1028.6 16.7 all-gather.6
  1050.5 16.5 all-gather.6
  1175.7 16.3 all-gather.6
  1565.2 1413.2 %while.39 = (s32[]{:T(128)}, f32[64,400]{1,0:T(8,128)S(1)}, f32[64,400]{1,0:T(8,128)S(1)}, bf16[70,64,400]{2,1,0:T(8,128)(2,1)}, f32[70,64,400]{2,1,0:T(8,128)},...) while((s32[]{:T(128)}, f32[64,400]{1,0:T(8,128)S(1)}, ...), condition=%wide.region_9.10_spmd.clone, body=%wide.region_7.9_spmd.clone.sunk | while | flops 21273604 | bytes 4586163 | solution.py:131
  1569.6 16.9 all-gather.7
  1651.4 16.3 all-gather.7
  1672.1 16.6 all-gather.7
  1693.1 16.3 all-gather.7
  1914.3 16.2 all-gather.7
  1935.0 16.5 all-gather.7
  2016.5 16.2 all-gather.7
  2037.1 16.7 all-gather.7
  2138.9 16.3 all-gather.7
  2159.6 16.6 all-gather.7
  2180.7 16.3 all-gather.7
  2403.4 16.7 all-gather.7
  2424.5 16.3 all-gather.7
  2647.3 16.7 all-gather.7
  2668.4 16.3 all-gather.7
  3031.3 16.5 fusion.34
  3067.1 48.0 %all-reduce.7.cloned.1.call-done = (f32[1,400,1150]{2,1,0:T(8,128)}, f32[1,400,400]{2,1,0:T(8,128)}) async-done(((f32[1,400,1150]{2,1,0:T(8,128)}, f32[1,400,400]{2,1,0:T(8,128)}), (f32[1,400,1150]{2,1,0:T(8,128)}, f32[1,400,400]{2,1,0:T(8,128)})) %all-reduce.7.cloned.1.call-update) | async-done | bytes 2480016 | tf_op jit(solution)/shard_map/psum | solution.py:167
  3120.5 17.5 concatenate.28
  3148.5 18.6 psum.39
  3167.0 233.9 %reduce-scatter.4.cloned.1.call-done = f32[16,70,1150]{2,1,0:T(8,128)} async-done(((f32[64,70,1150]{2,1,0:T(8,128)}), f32[16,70,1150]{2,1,0:T(8,128)}) %reduce-scatter.4.cloned.1.call-update) | async-done | bytes 5152016 | tf_op jit(solution)/shard_map/reduce_scatter | solution.py:155
  (1311 shorter events, 2383.2 us)
Async XLA Ops:
  8.0 13.6 copy-start
  8.0 3008.5 %reduce-scatter.8.cloned.1.call-start = ((), (), s32[]{:S(2)}) async-start(), calls=%async_computation.5 | async-start | bytes 2457600 | tf_op jit(solution)/shard_map/reduce_scatter | solution.py:164
  10.7 10.7 copy-start.4
  10.7 10.7 copy-start.6
  10.7 10.9 copy-start.10
  32.9 1468.5 %copy-start.11 = (s32[64]{0:T(128)S(1)}, s32[64]{0:T(128)}, u32[]{:S(2)}) copy-start(s32[64]{0:T(128)} %param.18) | copy-start | bytes 772
  1501.6 25.0 copy-start.9
  1533.7 4.6 copy-start.7
  2978.4 7.5 copy-start.1
  2978.4 7.4 copy-start.5
  2993.0 38.0 %reduce-scatter.6.cloned.1.call-start = ((), (), s32[]{:S(2)}) async-start(), calls=%async_computation.4 | async-start | bytes 5529600 | tf_op jit(solution)/shard_map/reduce_scatter | solution.py:163
  3016.4 98.7 %all-reduce.7.cloned.1.call-start = ((), (), s32[]{:S(2)}) async-start(), calls=%async_computation.6 | async-start | bytes 5324800 | tf_op jit(solution)/shard_map/psum | solution.py:167
  3031.0 370.0 %reduce-scatter.4.cloned.1.call-start = ((), (), s32[]{:S(2)}) async-start(), calls=%async_computation.3 | async-start | bytes 26542080 | tf_op jit(solution)/shard_map/reduce_scatter | solution.py:155
  3047.8 0.7 copy-start.12
  3067.1 336.8 %copy-start.8 = (f32[1,400]{1,0:T(1,128)}, f32[1,400]{1,0:T(1,128)S(1)}, u32[]{:S(2)}) copy-start(f32[1,400]{1,0:T(1,128)S(1)} %psum.38) | copy-start | bytes 4804
  3140.9 3.1 collective-permute-start
  3167.0 240.1 %copy-start.2 = (f32[1,400,1150]{2,1,0:T(8,128)S(1)}, f32[1,400,1150]{2,1,0:T(8,128)}, u32[]{:S(2)}) copy-start(f32[1,400,1150]{2,1,0:T(8,128)} %get-tuple-element.655) | copy-start | bytes 5520004
  3403.8 4.5 copy-start.3
Sparse Core Ops, SparseCore 0:
  2993.1 12.1 reduce-scatter.7
  3016.5 14.4 reduce-scatter.5
  3034.5 80.5 all-reduce.6
Sparse Core Ops, SparseCore 1:
  3047.9 353.0 reduce-scatter.3
